TPU v7x, 32 devices: a whole 2x2x4 slice. The times are simulated.
32 devices in a mesh: tm: 16 (over z, x, core), grid: 2 (over y).
Axes of the slice: x: 2, y: 2, z: 4, core: 2. Of those that a mesh axis runs over, the one named last changes fastest.
Arguments:
- times: float32 [8192], P(('tm', 'grid')), as said below
- cell_row: int32 [8192], P(('tm', 'grid')), may hold values from 0 to 127
- cell_col: int32 [8192], P(('tm', 'grid')), may hold values from 0 to 16383
- magnitude: int32 [8192], P(('tm', 'grid')), may hold values from 0 to 7
- base_rate: float32 [8192], P(('tm', 'grid')), may hold values from 0.02 to 0.2
- productivity: float32 [8], replicated, may hold values from 0.05 to 5
- spread: float32 [8], replicated, may hold values from 0.8 to 4.8
Outputs:
- log_event_intensity: float32 [8192], P(('tm', 'grid'))
- density: float32 [128, 16384], P(('tm', 'grid'))
Inputs may be any that keep to these rules, and one draw needn't show every extreme that they name: `times`: never decreasing along the events.
All inputs are finite; a program needn't handle non-finite values.
Results may differ from a plain program's by a relative error of at most 0.003.
Values sent between devices are 32-bit elements; how exact they have to be, the bound alone decides.
No kernel may reach another device: no remote copies, remote signals or barrier semaphores. Data moves between devices by JAX's collectives and lax.ppermute only.
A program may use at most 64 MiB of HBM per device.

v0:
```python
import math

import jax
import jax.numpy as jnp
from jax import lax
from jax.sharding import PartitionSpec as P

NB = 2
LATITUDE_SPAN = 4
COLS = 16384


omori_power = 1.2
omori_offset = 0.5
cell_km = 0.1
smooth_sigma = 1.5
rim_width = 3


def passed_along(shard, axis, by):
    size = lax.axis_size(axis)
    pairs = [(i, i + by) for i in range(size) if 0 <= i + by < size]
    return lax.ppermute(shard, axis, pairs)


def padded_2(cells, sides, width):
    for axis, dim in sides:
        count = lax.axis_size(axis)
        ends = count - 1
        head = lax.slice_in_dim(cells, 0, width, axis=dim)
        tail = lax.slice_in_dim(cells, cells.shape[dim] - width, cells.shape[dim], axis=dim)
        cells = jnp.concatenate(
            [
                lax.ppermute(tail, axis, [(i, (i + 1) % count) for i in range(ends)]),
                cells,
                lax.ppermute(head, axis, [((i + 1) % count, i) for i in range(ends)]),
            ],
            axis=dim,
        )
    return cells


def table_lookup(table, magnitude):
    onehot = (magnitude[None, :] == jnp.arange(table.shape[0], dtype=jnp.int32)[:, None]).astype(
        jnp.float32
    )
    return jnp.sum(table[:, None] * onehot, axis=0)


def pair_terms(target, source, keep_mask):
    gap_time = target[0][:, None] - source[0][None, :]
    gap_time = jnp.where(keep_mask, gap_time, 0.0)
    row_gap = target[1][:, None] - source[1][None, :]
    col_gap = target[2][:, None] - source[2][None, :]
    squared = (row_gap * row_gap + col_gap * col_gap) * (cell_km * cell_km)
    contrib = source[3][None, :] * jnp.exp(
        -omori_power * jnp.log(gap_time + omori_offset) - squared * source[4][None, :]
    )
    return jnp.sum(jnp.where(keep_mask, contrib, 0.0), axis=1)


def smooth_weights():
    offsets = jnp.arange(-rim_width, rim_width + 1).astype(jnp.float32)
    weights = jnp.exp(-offsets * offsets / (2.0 * smooth_sigma * smooth_sigma))
    return weights / jnp.sum(weights)


def column_pass(values, weights):
    length = values.shape[1]
    padded = jnp.pad(values, ((0, 0), (rim_width, rim_width)))
    summed = weights[0] * padded[:, 0:length]
    for offset in range(1, 2 * rim_width + 1):
        summed = summed + weights[offset] * padded[:, offset : offset + length]
    return summed


def row_pass(values, weights, length):
    summed = weights[0] * values[0:length]
    for offset in range(1, 2 * rim_width + 1):
        summed = summed + weights[offset] * values[offset : offset + length]
    return summed


def make_depositor(first_row, slab_rows, running, shard_piece):
    local_rows = shard_piece[0].astype(jnp.int32) - first_row
    inside = (local_rows >= 0) & (local_rows < slab_rows)
    safe_rows = jnp.where(inside, local_rows, slab_rows)
    col_index = shard_piece[1].astype(jnp.int32)
    return running.at[safe_rows, col_index].add(shard_piece[2], mode="drop")


def body(times, cell_row, cell_col, magnitude, base_rate, productivity, spread):
    events_here = times.shape[0]
    producing = table_lookup(productivity, magnitude)
    sigma_km = table_lookup(spread, magnitude)
    normalizing_factor = (omori_power - 1.0) * omori_offset ** (omori_power - 1.0)
    amplitude = producing * normalizing_factor / (2.0 * math.pi * sigma_km * sigma_km)
    inverse = 1.0 / (2.0 * sigma_km * sigma_km)
    row_float = cell_row.astype(jnp.float32)
    col_float = cell_col.astype(jnp.float32)
    payload = jnp.stack([times, row_float, col_float, amplitude, inverse])
    earlier = []
    current = payload
    for offset in range(NB):
        current = passed_along(current, ("tm", "grid"), 1)
        earlier.append(current)
    target_rows = min(512, events_here)
    target_blocks = events_here // target_rows
    position = jnp.arange(events_here, dtype=jnp.int32)

    def block_sum(target_block):
        first_event = target_block * target_rows
        target_ids = first_event + jnp.arange(target_rows, dtype=jnp.int32)
        causal = position[None, :] < target_ids[:, None]
        summed = pair_terms(payload, payload, causal)
        for source in earlier:
            summed = summed + pair_terms(payload, source, True)
        return summed

    trigger = lax.map(block_sum, jnp.arange(target_blocks, dtype=jnp.int32)).reshape(-1)
    intensity = base_rate + trigger
    log_event_intensity = jnp.log(intensity)
    share = (base_rate / intensity).astype(jnp.bfloat16)
    cell_payload = jnp.stack([row_float, col_float, share.astype(jnp.float32)])
    pair_count = lax.axis_size("grid")
    first_row = lax.axis_index("tm") * (pair_count * LATITUDE_SPAN)
    empty_pair = jnp.zeros((pair_count * LATITUDE_SPAN, COLS), jnp.float32)
    pair_grid = make_depositor(
        first_row,
        pair_count * LATITUDE_SPAN,
        empty_pair,
        lax.all_gather(cell_payload, "tm", axis=1, tiled=True),
    )
    raw_grid = lax.psum_scatter(pair_grid, "grid", scatter_dimension=0, tiled=True)
    weights = smooth_weights()
    extended = padded_2(raw_grid, ((("tm", "grid"), 0),), rim_width)
    across = column_pass(extended, weights)
    density = row_pass(across, weights, LATITUDE_SPAN)
    return (log_event_intensity, density)


def solution(mesh):
    in_specs = (
        P(("tm", "grid")),
        P(("tm", "grid")),
        P(("tm", "grid")),
        P(("tm", "grid")),
        P(("tm", "grid")),
        P(),
        P(),
    )
    out_specs = (P(("tm", "grid")), P(("tm", "grid"), None))
    return jax.shard_map(body, mesh=mesh, in_specs=in_specs, out_specs=out_specs, check_vma=False)
```

profile of v0, /device:TPU:0, one launch (start us, length us, event | category | flops | bytes accessed | tf_op | source)
XLA Modules:
  0.0 129.8 jit_solution(1887690312700865415)
XLA Ops:
  7.2 0.0 all-reduce.4.cloned.1.call-start
  7.2 0.7 convert_element_type.43
  7.9 0.7 convert_element_type.44
  8.6 0.8 select_reduce_fusion.1
  9.4 0.7 stack.28
  10.1 4.9 %collective-permute-start = (f32[5,256]{1,0:T(8,128)S(1)}, f32[5,256]{1,0:T(8,128)S(1)}, u32[]{:S(2)}, u32[]{:S(2)}) collective-permute-start(f32[5,256]{1,0:T(8,128)S(1)} %stack.28), channel_id=1, source_target_pairs={{0,1},{1,2},{2,3},{3,4},{4,5},{5,6},{6,7},{7,8},{8,9},{9,10},{10,1... | collective-permute-start | bytes 15368 | tf_op jit(solution)/shard_map/ppermute | solution.py:23
  15.0 1.3 %collective-permute-done = f32[5,256]{1,0:T(8,128)S(1)} collective-permute-done((f32[5,256]{1,0:T(8,128)S(1)}, f32[5,256]{1,0:T(8,128)S(1)}, u32[]{:S(2)}, u32[]{:S(2)}) %collective-permute-start) | collective-permute-done | bytes 5152 | tf_op jit(solution)/shard_map/ppermute | solution.py:23
  16.4 4.2 %collective-permute-start.1 = (f32[5,256]{1,0:T(8,128)S(1)}, f32[5,256]{1,0:T(8,128)S(1)}, u32[]{:S(2)}, u32[]{:S(2)}) collective-permute-start(f32[5,256]{1,0:T(8,128)S(1)} %collective-permute-done), channel_id=1, source_target_pairs={{0,1},{1,2},{2,3},{3,4},{4,5},{5,6},{6,7},{7,8},{8,9},{9,10},{10,1... | collective-permute-start | bytes 15368 | tf_op jit(solution)/shard_map/ppermute | solution.py:23
  20.6 1.3 %collective-permute-done.1 = f32[5,256]{1,0:T(8,128)S(1)} collective-permute-done((f32[5,256]{1,0:T(8,128)S(1)}, f32[5,256]{1,0:T(8,128)S(1)}, u32[]{:S(2)}, u32[]{:S(2)}) %collective-permute-start.1) | collective-permute-done | bytes 5152 | tf_op jit(solution)/shard_map/ppermute | solution.py:23
  21.9 1.3 multiply_reduce_fusion.1
  23.2 1.3 fusion.21
  24.5 23.2 %all_gather.3 = f32[3,4096]{1,0:T(4,128)S(1)} all-gather(f32[3,256]{1,0:T(4,128)S(1)} %pad_maximum_fusion.1), channel_id=1, replica_groups=mesh['tm'=16,'grid'=2] {'tm'}, dimensions={1}, use_global_device_ids=true | all-gather | bytes 52224 | tf_op jit(solution)/shard_map/all_gather | solution.py:132
  47.7 0.1 compare_select_fusion.1
  47.8 0.1 and_reduce_fusion
  47.9 0.1 multiply_reduce_fusion.2
  48.1 22.0 %scatter_custom_fusion = f32[131072]{0:T(1024)S(1)} fusion(s32[4096]{0:T(1024)S(1)} %broadcast_select_fusion, f32[4096]{0:T(1024)S(1)} %bitcast.33, f32[]{:T(128)} %constant.18.clone.1), kind=kCustom, calls=%fused_computation.21 | custom fusion | flops 4096 | bytes 524292
  70.1 0.9 reshape.118
  71.0 0.0 all-reduce.4.cloned.1.call-update
  71.0 0.6 dynamic-slice
  72.3 0.6 fusion.22
  72.9 0.7 broadcast_divide_fusion
  73.6 0.7 fusion.26
  74.2 22.3 %all-reduce.4.cloned.1.call-done = f32[8,16384]{1,0:T(8,128)} async-done(((f32[8,16384]{1,0:T(8,128)}), f32[8,16384]{1,0:T(8,128)}) %all-reduce.4.cloned.1.call-update) | async-done | bytes 524304
  96.5 1.4 %constant_dynamic-slice_fusion.1 = (f32[3,16384]{1,0:T(4,128)S(1)}, f32[3,16384]{1,0:T(4,128)S(1)}) fusion(f32[8,16384]{1,0:T(8,128)} %all-reduce.4.cloned.1.call-done, u32[]{:T(128)S(6)} %add.143, u32[]{:T(128)S(6)} %multiply.11), kind=kLoop, calls=%fused_computation.55 | loop fusion | bytes 786440 | tf_op jit(solution)/shard_map/slice | solution.py:31
  97.8 2.3 %collective-permute-start.2 = (f32[3,16384]{1,0:T(4,128)S(1)}, f32[3,16384]{1,0:T(4,128)S(1)}, u32[]{:S(2)}, u32[]{:S(2)}) collective-permute-start(f32[3,16384]{1,0:T(4,128)S(1)} %get-tuple-element.33), channel_id=1, source_target_pairs={{0,1},{1,2},{2,3},{3,4},{4,5},{5,6},{6,7},{7,8},{8,9},{9,10},{10,1... | collective-permute-start | bytes 589832 | tf_op jit(solution)/shard_map/ppermute | solution.py:34
  100.1 1.3 collective-permute-start.3
  101.4 0.1 constant_dynamic-slice_fusion.2
  101.5 8.0 %collective-permute-done.2 = f32[3,16384]{1,0:T(4,128)S(1)} collective-permute-done((f32[3,16384]{1,0:T(4,128)S(1)}, f32[3,16384]{1,0:T(4,128)S(1)}, u32[]{:S(2)}, u32[]{:S(2)}) %collective-permute-start.2) | collective-permute-done | bytes 196640 | tf_op jit(solution)/shard_map/ppermute | solution.py:34
  109.4 1.7 %collective-permute-done.3 = f32[3,16384]{1,0:T(4,128)S(1)} collective-permute-done((f32[3,16384]{1,0:T(4,128)S(1)}, f32[3,16384]{1,0:T(4,128)S(1)}, u32[]{:S(2)}, u32[]{:S(2)}) %collective-permute-start.3) | collective-permute-done | bytes 196640 | tf_op jit(solution)/shard_map/ppermute | solution.py:36
  111.2 0.2 pad_maximum_fusion
  111.4 6.1 %multiply_add_fusion = f32[10,16384]{1,0:T(8,128)S(1)} fusion(f32[10,16384]{1,0:T(8,128)S(1)} %pad_maximum_fusion, f32[]{:T(128)} %bitcast.26, f32[]{:T(128)} %bitcast.25, f32[]{:T(128)} %bitcast.24, f32[]{:T(128)} %bitcast.23, f32[]{:T(128)} %bitcast.22, f32[]{:T(128)} %bitcast.21, f32[]{:T(128)} %bitcast.15), kind=kLoop, calls=%fused_computation.2 | loop fusion | flops 2129920 | bytes 1310748 | tf_op jit(solution)/shard_map/add | solution.py:73
  117.5 5.5 %fusion.3 = f32[4,16384]{1,0:T(4,128)} fusion(f32[10,16384]{1,0:T(8,128)S(1)} %multiply_add_fusion, f32[]{:T(128)} %bitcast.26, f32[]{:T(128)} %bitcast.25, f32[]{:T(128)} %bitcast.24, f32[]{:T(128)} %bitcast.23, f32[]{:T(128)} %bitcast.22, f32[]{:T(128)} %bitcast.21, f32[]{:T(128)} %bitcast.15), kind=kLoop, calls=%fused_computation.9 | loop fusion | flops 851968 | bytes 2097180 | tf_op jit(solution)/shard_map/add | solution.py:80
  (15 shorter events, 0.1 us)
Async XLA Ops:
  7.2 40.6 %copy-start.2 = (s32[2]{0:T(128)S(1)}, s32[2]{0:T(128)}, u32[]{:S(2)}) copy-start(s32[2]{0:T(128)} %constant.64) | copy-start | bytes 28
  7.2 40.7 %copy-start.1 = (s32[2]{0:T(128)S(1)}, s32[2]{0:T(128)}, u32[]{:S(2)}) copy-start(s32[2]{0:T(128)} %constant.61) | copy-start | bytes 28
  7.2 89.3 %all-reduce.4.cloned.1.call-start = ((), (), s32[]{:S(2)}) async-start(), calls=%async_computation | async-start | bytes 1048576
  10.1 6.3 %collective-permute-start = (f32[5,256]{1,0:T(8,128)S(1)}, f32[5,256]{1,0:T(8,128)S(1)}, u32[]{:S(2)}, u32[]{:S(2)}) collective-permute-start(f32[5,256]{1,0:T(8,128)S(1)} %stack.28), channel_id=1, source_target_pairs={{0,1},{1,2},{2,3},{3,4},{4,5},{5,6},{6,7},{7,8},{8,9},{9,10},{10,1... | collective-permute-start | bytes 15368 | tf_op jit(solution)/shard_map/ppermute | solution.py:23
  16.4 5.5 %collective-permute-start.1 = (f32[5,256]{1,0:T(8,128)S(1)}, f32[5,256]{1,0:T(8,128)S(1)}, u32[]{:S(2)}, u32[]{:S(2)}) collective-permute-start(f32[5,256]{1,0:T(8,128)S(1)} %collective-permute-done), channel_id=1, source_target_pairs={{0,1},{1,2},{2,3},{3,4},{4,5},{5,6},{6,7},{7,8},{8,9},{9,10},{10,1... | collective-permute-start | bytes 15368 | tf_op jit(solution)/shard_map/ppermute | solution.py:23
  48.0 23.0 %copy-start.3 = (u32[32]{0:T(128)S(1)}, u32[32]{0:T(128)}, u32[]{:S(2)}) copy-start(u32[32]{0:T(128)} %constant.71) | copy-start | bytes 388
  96.5 4.9 %copy-start = (f32[8,16384]{1,0:T(8,128)S(1)}, f32[8,16384]{1,0:T(8,128)}, u32[]{:S(2)}) copy-start(f32[8,16384]{1,0:T(8,128)} %all-reduce.4.cloned.1.call-done) | copy-start | bytes 1572868
  97.8 11.6 %collective-permute-start.2 = (f32[3,16384]{1,0:T(4,128)S(1)}, f32[3,16384]{1,0:T(4,128)S(1)}, u32[]{:S(2)}, u32[]{:S(2)}) collective-permute-start(f32[3,16384]{1,0:T(4,128)S(1)} %get-tuple-element.33), channel_id=1, source_target_pairs={{0,1},{1,2},{2,3},{3,4},{4,5},{5,6},{6,7},{7,8},{8,9},{9,10},{10,1... | collective-permute-start | bytes 589832 | tf_op jit(solution)/shard_map/ppermute | solution.py:34
  100.1 11.1 %collective-permute-start.3 = (f32[3,16384]{1,0:T(4,128)S(1)}, f32[3,16384]{1,0:T(4,128)S(1)}, u32[]{:S(2)}, u32[]{:S(2)}) collective-permute-start(f32[3,16384]{1,0:T(4,128)S(1)} %get-tuple-element.34), channel_id=1, source_target_pairs={{1,0},{2,1},{3,2},{4,3},{5,4},{6,5},{7,6},{8,7},{9,8},{10,9},{11,1... | collective-permute-start | bytes 589832 | tf_op jit(solution)/shard_map/ppermute | solution.py:36
Sparse Core Ops, SparseCore 0:
  71.2 25.2 all-reduce.3
where the time goes:
time: 131 us; the launch traced here: 130 us
  other arithmetic  40.2 us (31%)
  waiting for transfers between devices  34.6 us (26%)
  blocking collectives  23.2 us (18%)
  between operations  14.9 us (11%)
  starting transfers between devices  12.7 us (10%)
  local copies, waits for them, and re-layouts  4.3 us (3%)
    all_gather x1, blocking collectives, body(): lax.all_gather(cell_payload, 'tm', axis=1, tiled=True)  23.2 us
    unnamed x4, other arithmetic  22.3 us
    unnamed x2, waiting for transfers between devices  22.3 us
    ppermute x2, starting transfers between devices, passed_along(): return lax.ppermute(shard, axis, pairs)  9.07 us
    ppermute x1, waiting for transfers between devices, padded_2(): lax.ppermute(tail, axis, [(i, (i + 1) % count) for i in range(ends)])  7.96 us
    add x1, other arithmetic, column_pass(): summed = summed + weights[offset] * padded[:, offset:offset + length]  6.06 us
    add x1, other arithmetic, row_pass(): summed = summed + weights[offset] * values[offset:offset + length]  5.51 us
    ppermute x2, waiting for transfers between devices, passed_along(): return lax.ppermute(shard, axis, pairs)  2.68 us
  transfers between devices with their start and end apart: 5, of which 5 were waited for; matrix products, arithmetic and copies ran while one was open for 2% of the time, Pallas kernels for 0%

commit v1 on v0

v1 whole, which is shorter than its diff:
```python
import functools
import math

import jax
import jax.numpy as jnp
from jax import lax
from jax.experimental import pallas as pl
from jax.experimental.pallas import tpu as pltpu
from jax.sharding import PartitionSpec as P

NB = 2
LATITUDE_SPAN = 4
COLS = 16384

omori_power = 1.2
omori_offset = 0.5
cell_km = 0.1
smooth_sigma = 1.5
rim_width = 3

AXES = ("tm", "grid")
CHUNK = 32
LOG2E = math.log2(math.e)
WEIGHTS = [math.exp(-(b * b) / (2.0 * smooth_sigma**2)) for b in range(-rim_width, rim_width + 1)]
WEIGHT_SUM = sum(WEIGHTS)


def kernel(g_ref, prod_ref, spread_ref, logint_ref, dens_ref,
           t_s, r_s, c_s, l_s, v_s, b_s, pos_s, posm_s, cnt_v, cnt_s, a_buf, b_buf, x_s, sem):
    blocks = g_ref.shape[0]
    events = g_ref.shape[1] // 5
    nbin = prod_ref.shape[0]
    lo_cols = b_buf.shape[1]
    m_rows = a_buf.shape[1]
    batch = a_buf.shape[0]
    per_batch = batch // CHUNK
    own = lax.axis_index("tm") * lax.axis_size("grid") + lax.axis_index("grid")
    first_row = (own * LATITUDE_SPAN).astype(jnp.float32)

    times = g_ref[:, 0:events]
    rows = g_ref[:, events : 2 * events]
    mag = g_ref[:, 3 * events : 4 * events]
    t_s[0:blocks] = times
    r_s[0:blocks] = rows
    c_s[0:blocks] = g_ref[:, 2 * events : 3 * events]
    b_s[...] = g_ref[:, 4 * events : 5 * events]
    producing = jnp.full_like(mag, prod_ref[0])
    sigma = jnp.full_like(mag, spread_ref[0])
    for k in range(1, nbin):
        hit = mag == float(k)
        producing = jnp.where(hit, prod_ref[k], producing)
        sigma = jnp.where(hit, spread_ref[k], sigma)
    norm = (omori_power - 1.0) * omori_offset ** (omori_power - 1.0) / (2.0 * math.pi)
    area = sigma * sigma
    l_s[0:blocks] = jnp.log(producing * norm / area) * LOG2E
    v_s[0:blocks] = (0.5 * cell_km * cell_km * LOG2E) / area
    pad = (8, events)
    t_s[blocks : blocks + 8] = jnp.broadcast_to(times[0:1, 0:1], pad)
    r_s[blocks : blocks + 8] = jnp.zeros(pad, jnp.float32)
    c_s[blocks : blocks + 8] = jnp.zeros(pad, jnp.float32)
    l_s[blocks : blocks + 8] = jnp.full(pad, -1e30, jnp.float32)
    v_s[blocks : blocks + 8] = jnp.zeros(pad, jnp.float32)

    need = (rows >= first_row - rim_width) & (rows <= first_row + (LATITUDE_SPAN - 1 + rim_width))
    need_b = jnp.where(need, 1.0, 0.0).astype(jnp.bfloat16)
    upper = (
        lax.broadcasted_iota(jnp.int32, (events, events), 0)
        <= lax.broadcasted_iota(jnp.int32, (events, events), 1)
    )
    upper = jnp.where(upper, 1.0, 0.0).astype(jnp.bfloat16)
    pos = jnp.dot(need_b, upper, preferred_element_type=jnp.float32)
    pos_s[0:blocks] = pos
    posm_s[0:blocks] = jnp.where(need, pos, 0.0)
    ident = lax.broadcasted_iota(jnp.int32, pad, 1).astype(jnp.float32) + 1.0
    pos_s[blocks : blocks + 8] = ident
    posm_s[blocks : blocks + 8] = ident
    counts = lax.dot_general(
        jnp.ones((8, events), jnp.bfloat16), need_b, (((1,), (1,)), ((), ())),
        preferred_element_type=jnp.float32,
    )
    cnt_v[...] = counts.astype(jnp.int32)
    copy = pltpu.make_async_copy(cnt_v, cnt_s, sem)
    copy.start()

    rank = lax.broadcasted_iota(jnp.int32, (CHUNK, events), 0).astype(jnp.float32) + 1.0

    def row_of(ref, b):
        return ref[pl.ds(b, 1), :]

    def triggers(b, prow, first):
        order = rank + first
        pick = row_of(posm_s, prow) == order

        def taken(ref):
            return jnp.sum(jnp.where(pick, row_of(ref, b), 0.0), axis=1, keepdims=True)

        t_i, r_i, c_i, b_i = taken(t_s), taken(r_s), taken(c_s), taken(b_s)
        total = None
        for back in range(NB + 1):
            s = b if back == 0 else jnp.where(b >= back, b - back, blocks)
            gap = (t_i - row_of(t_s, s)) + omori_offset
            dr = r_i - row_of(r_s, s)
            dc = c_i - row_of(c_s, s)
            expo = (row_of(l_s, s) - (omori_power * LOG2E) * jnp.log(gap)) - (
                dr * dr + dc * dc
            ) * row_of(v_s, s)
            term = jnp.exp2(expo)
            if back == 0:
                term = jnp.where(row_of(pos_s, prow) < order, term, 0.0)
            total = term if total is None else total + term
        return pick, r_i, c_i, b_i, jnp.sum(total, axis=1, keepdims=True)

    lane_m = lax.broadcasted_iota(jnp.int32, (CHUNK, m_rows), 1)
    m_row = (lane_m % LATITUDE_SPAN).astype(jnp.float32)
    m_hi = (lane_m // LATITUDE_SPAN).astype(jnp.float32)
    lane_l = lax.broadcasted_iota(jnp.int32, (CHUNK, lo_cols), 1).astype(jnp.float32)

    def deposit(b, first, slot):
        _, r_i, c_i, b_i, trig = triggers(b, b, first)
        share = jnp.where(b_i > 0.0, b_i / (b_i + trig), 0.0)
        share = share.astype(jnp.bfloat16).astype(jnp.float32)
        hi = jnp.floor(c_i * (1.0 / lo_cols))
        lo = c_i - hi * lo_cols
        d = m_row - (r_i - first_row)
        d2 = d * d
        w = jnp.exp2(d2 * (-LOG2E / (2.0 * smooth_sigma**2))) * (share * (1.0 / WEIGHT_SUM))
        a = jnp.where((m_hi == hi) & (d2 < (rim_width + 0.5) ** 2), w, 0.0)
        a_buf[pl.ds(slot, CHUNK), :] = a.astype(jnp.bfloat16)
        b_buf[pl.ds(slot, CHUNK), :] = jnp.where(lane_l == lo, 1.0, 0.0).astype(jnp.bfloat16)

    def flush():
        x_s[8 : 8 + m_rows] += lax.dot_general(
            a_buf[...], b_buf[...], (((0,), (0,)), ((), ())), preferred_element_type=jnp.float32
        )

    x_s[...] = jnp.zeros_like(x_s)

    def batch_step(i, carry):
        for j in range(per_batch):
            deposit(i * per_batch + j, 0.0, j * CHUNK)
        flush()
        return carry

    lax.fori_loop(0, blocks // per_batch, batch_step, 0)

    out_row = jnp.zeros((1, events), jnp.float32)
    for k in range(events // CHUNK):
        pick, _, _, _, trig = triggers(own, blocks, float(k * CHUNK))
        out_row = out_row + jnp.sum(jnp.where(pick, trig, 0.0), axis=0, keepdims=True)
    logint_ref[...] = jnp.log(row_of(b_s, own) + out_row)

    copy.wait()
    a_buf[...] = jnp.zeros_like(a_buf)

    def extra_block(b, slot):
        def extra(c, slot):
            deposit(b, (c * CHUNK).astype(jnp.float32), pl.multiple_of(slot, CHUNK))
            slot = slot + CHUNK

            @pl.when(slot == batch)
            def _():
                flush()
                a_buf[...] = jnp.zeros_like(a_buf)

            return jnp.where(slot == batch, 0, slot)

        return lax.fori_loop(1, (cnt_s[0, b] + (CHUNK - 1)) // CHUNK, extra, slot)

    left = lax.fori_loop(0, blocks, extra_block, 0)

    @pl.when(left > 0)
    def _():
        flush()

    span = LATITUDE_SPAN
    mid = x_s[8 : 8 + m_rows]
    before = x_s[8 - span : 8 - span + m_rows]
    after = x_s[8 + span : 8 + span + m_rows]
    lane = lax.broadcasted_iota(jnp.int32, (m_rows, lo_cols), 1)
    acc = mid * (WEIGHTS[rim_width] / WEIGHT_SUM)
    for b in range(1, rim_width + 1):
        from_left = jnp.where(lane < b, pltpu.roll(before, b, 1), pltpu.roll(mid, b, 1))
        from_right = jnp.where(
            lane >= lo_cols - b, pltpu.roll(after, lo_cols - b, 1), pltpu.roll(mid, lo_cols - b, 1)
        )
        acc = acc + (from_left + from_right) * (WEIGHTS[rim_width + b] / WEIGHT_SUM)
    for h in range(m_rows // span):
        dens_ref[:, h * lo_cols : (h + 1) * lo_cols] = acc[h * span : (h + 1) * span]


def body(times, cell_row, cell_col, magnitude, base_rate, productivity, spread):
    events = times.shape[0]
    count = lax.axis_size(AXES)
    f32 = jnp.float32
    payload = jnp.concatenate(
        [times, cell_row.astype(f32), cell_col.astype(f32), magnitude.astype(f32), base_rate]
    )
    gathered = lax.all_to_all(
        jnp.broadcast_to(payload[None], (count, payload.shape[0])), AXES, 0, 0, tiled=True
    )
    lo_cols = 256
    m_rows = LATITUDE_SPAN * (COLS // lo_cols)
    per_batch = math.gcd(count, 8)
    field = pltpu.VMEM((count + 8, events), f32)
    log_intensity, density = pl.pallas_call(
        kernel,
        out_shape=(
            jax.ShapeDtypeStruct((1, events), f32),
            jax.ShapeDtypeStruct((LATITUDE_SPAN, COLS), f32),
        ),
        in_specs=[
            pl.BlockSpec(memory_space=pltpu.VMEM),
            pl.BlockSpec(memory_space=pltpu.SMEM),
            pl.BlockSpec(memory_space=pltpu.SMEM),
        ],
        out_specs=(
            pl.BlockSpec(memory_space=pltpu.VMEM),
            pl.BlockSpec(memory_space=pltpu.VMEM),
        ),
        scratch_shapes=[
            field, field, field, field, field,
            pltpu.VMEM((count, events), f32),
            field, field,
            pltpu.VMEM((8, count), jnp.int32),
            pltpu.SMEM((8, count), jnp.int32),
            pltpu.VMEM((per_batch * CHUNK, m_rows), jnp.bfloat16),
            pltpu.VMEM((per_batch * CHUNK, lo_cols), jnp.bfloat16),
            pltpu.VMEM((m_rows + 16, lo_cols), f32),
            pltpu.SemaphoreType.DMA,
        ],
    )(gathered, productivity, spread)
    return (log_intensity.reshape(events), density)


def solution(mesh):
    in_specs = (P(AXES), P(AXES), P(AXES), P(AXES), P(AXES), P(), P())
    out_specs = (P(AXES), P(AXES, None))
    return jax.shard_map(body, mesh=mesh, in_specs=in_specs, out_specs=out_specs, check_vma=False)
```

time: 131 us -> 29.1 us (0.22)
  other arithmetic: 40.2 us -> 0.02 us
  waiting for transfers between devices: 34.6 us -> 0 us
  between operations: 14.9 us -> 0.66 us
  starting transfers between devices: 12.7 us -> 0 us
  Pallas kernels: 0 us -> 7.81 us
  blocking collectives: 23.2 us -> 16.2 us
    all_gather x1 -> x0, blocking collectives: 23.2 us -> none  [body(): lax.all_gather(cell_payload, 'tm', axis=1, tiled=True)]
    unnamed x2 -> x0, waiting for transfers between devices: 22.3 us -> none
    unnamed x4, other arithmetic: 22.3 us -> 0.02 us
    all_to_all x0 -> x1, blocking collectives: none -> 16.2 us  [body(): lax.all_to_all(jnp.broadcast_to(payload[None], (count, payload.shape[0]))...]
    ppermute x4 -> x0, starting transfers between devices: 12.6 us -> none  [the longest x2 9.07 us: passed_along(): return lax.ppermute(shard, axis, pairs)]
    ppermute x4 -> x0, waiting for transfers between devices: 12.4 us -> none  [the longest x1 7.96 us: padded_2(): lax.ppermute(tail, axis, [(i, (i + 1) % count) for i in range(ends)])]
    add x2 -> x0, other arithmetic: 11.6 us -> none  [the longest x1 6.06 us: column_pass(): summed = summed + weights[offset] * padded[:, offset:offset + length]]
    pallas_call x0 -> x1, Pallas kernels: none -> 7.81 us  [body(): pl.pallas_call(kernel, out_shape=(jax.ShapeDtypeStruct((1, events), f32),...]
  transfers between devices with their start and end apart: 5 -> 0, of which waited for: 5 -> 0; matrix products, arithmetic and copies ran while one was open for 2% -> 0% of each run, Pallas kernels for 0% -> 0%
where the time goes in v1:
time: 29.1 us; the launch traced here: 28.8 us
  blocking collectives  16.2 us (56%)
  Pallas kernels  7.81 us (27%)
  local copies, waits for them, and re-layouts  4.12 us (14%)
  between operations  0.66 us (2%)
    all_to_all x1, blocking collectives, body(): lax.all_to_all(jnp.broadcast_to(payload[None], (count, payload.shape[0]))...  16.2 us
    pallas_call x1, Pallas kernels, body(): pl.pallas_call(kernel, out_shape=(jax.ShapeDtypeStruct((1, events), f32),...  7.81 us
    unnamed x12, local copies, waits for them, and re-layouts  4.03 us

profile of v1, /device:TPU:0, one launch (start us, length us, event | category | flops | bytes accessed | tf_op | source)
XLA Modules:
  0.0 28.8 jit_solution(5053224948865587429)
XLA Ops:
  0.6 0.0 copy-start
  0.6 0.7 %copy-done = f32[256]{0:T(256)S(1)} copy-done((f32[256]{0:T(256)S(1)}, f32[256]{0:T(256)}, u32[]{:S(2)}) %copy-start) | copy-done | bytes 1048
  1.3 0.0 copy-start.1
  1.3 0.7 %copy-done.1 = s32[256]{0:T(256)S(1)} copy-done((s32[256]{0:T(256)S(1)}, s32[256]{0:T(256)}, u32[]{:S(2)}) %copy-start.1) | copy-done | bytes 1048
  2.0 0.0 copy-start.2
  2.0 0.7 %copy-done.2 = s32[256]{0:T(256)S(1)} copy-done((s32[256]{0:T(256)S(1)}, s32[256]{0:T(256)}, u32[]{:S(2)}) %copy-start.2) | copy-done | bytes 1048
  2.7 0.0 copy-start.3
  2.7 0.7 %copy-done.3 = s32[256]{0:T(256)S(1)} copy-done((s32[256]{0:T(256)S(1)}, s32[256]{0:T(256)}, u32[]{:S(2)}) %copy-start.3) | copy-done | bytes 1048
  3.3 0.0 copy-start.4
  3.4 0.7 %copy-done.4 = f32[256]{0:T(256)S(1)} copy-done((f32[256]{0:T(256)S(1)}, f32[256]{0:T(256)}, u32[]{:S(2)}) %copy-start.4) | copy-done | bytes 1048
  4.0 0.1 broadcast_in_dim.2
  4.1 16.2 %all_to_all.8 = f32[32,1,1280]{2,1,0:T(1,128)S(1)} all-to-all(f32[32,1,1280]{2,1,0:T(1,128)S(1)} %broadcast_in_dim.2), channel_id=1, replica_groups=mesh['tm'=16,'grid'=2] {'tm','grid'}, dimensions={0} | all-to-all | bytes 327680 | tf_op jit(solution)/shard_map/all_to_all | solution.py:198
  20.4 0.7 %copy.11 = f32[32,1,1280]{2,0,1:T(8,128)} copy(f32[32,1,1280]{2,1,0:T(1,128)S(1)} %all_to_all.8) | data formatting | bytes 327680
  21.0 7.8 %shard_map.86 = (f32[1,256]{1,0:T(1,128)}, f32[4,16384]{1,0:T(4,128)}) custom-call(f32[32,1280]{1,0:T(8,128)} %bitcast.4, f32[8]{0:T(128)} %prod_ref.1, f32[8]{0:T(128)} %spread_ref.1), custom_call_target="tpu_custom_call" | custom-call | tf_op jit(solution)/shard_map/pallas_call | solution.py:205
  (6 shorter events, 0.0 us)
Async XLA Ops:
  0.6 0.7 %copy-start = (f32[256]{0:T(256)S(1)}, f32[256]{0:T(256)}, u32[]{:S(2)}) copy-start(f32[256]{0:T(256)} %param.7) | copy-start | bytes 3076
  1.3 0.7 %copy-start.1 = (s32[256]{0:T(256)S(1)}, s32[256]{0:T(256)}, u32[]{:S(2)}) copy-start(s32[256]{0:T(256)} %param.8) | copy-start | bytes 3076
  2.0 0.7 %copy-start.2 = (s32[256]{0:T(256)S(1)}, s32[256]{0:T(256)}, u32[]{:S(2)}) copy-start(s32[256]{0:T(256)} %param.9) | copy-start | bytes 3076
  2.7 0.7 %copy-start.3 = (s32[256]{0:T(256)S(1)}, s32[256]{0:T(256)}, u32[]{:S(2)}) copy-start(s32[256]{0:T(256)} %param.10) | copy-start | bytes 3076
  3.3 0.7 %copy-start.4 = (f32[256]{0:T(256)S(1)}, f32[256]{0:T(256)}, u32[]{:S(2)}) copy-start(f32[256]{0:T(256)} %param.11) | copy-start | bytes 3076

commit v2 on v1

v2 whole, which is shorter than its diff:
```python
import math

import jax
import jax.numpy as jnp
from jax import lax
from jax.experimental import pallas as pl
from jax.experimental.pallas import tpu as pltpu
from jax.sharding import PartitionSpec as P

NB = 2
LATITUDE_SPAN = 4
COLS = 16384

omori_power = 1.2
omori_offset = 0.5
cell_km = 0.1
smooth_sigma = 1.5
rim_width = 3

AXES = ("tm", "grid")
LANES = 128
UNIT = 8
STEP = 8
BATCH = 256
LO_COLS = 256
M_ROWS = LATITUDE_SPAN * (COLS // LO_COLS)
LOG2E = math.log2(math.e)
WEIGHTS = [math.exp(-(b * b) / (2.0 * smooth_sigma**2)) for b in range(-rim_width, rim_width + 1)]
WEIGHT_SUM = sum(WEIGHTS)
MIB = 1 << 20


def spread_kernel(t_ref, r_ref, c_ref, m_ref, b_ref, out_ref):
    events = t_ref.shape[1]
    shape = (out_ref.shape[0], 1, events)
    for k, ref in enumerate([t_ref, r_ref, c_ref, m_ref, b_ref]):
        row = ref[...].astype(jnp.float32)
        out_ref[:, :, k * events : (k + 1) * events] = jnp.broadcast_to(row[None], shape)


def kernel(g_ref, prod_ref, spread_ref, logint_ref, dens_ref,
           t_s, r_s, c_s, l_s, v_s, b_s, pos_s, posm_s,
           blk_v, fst_v, blk_s, fst_s, sel_s, dep_s, a_buf, b_buf, x_s, sems):
    f32 = jnp.float32
    bf16 = jnp.bfloat16
    blocks = g_ref.shape[0]
    events = g_ref.shape[2] // 5
    halves = events // LANES
    nbin = prod_ref.shape[0]
    listed = blk_v.shape[1]
    own = lax.axis_index("tm") * lax.axis_size("grid") + lax.axis_index("grid")
    first_row = (own * LATITUDE_SPAN).astype(f32)

    times = g_ref[:, 0, 0:events]
    rows = g_ref[:, 0, events : 2 * events]
    mag = g_ref[:, 0, 3 * events : 4 * events]

    need = (rows >= first_row - rim_width) & (rows <= first_row + (LATITUDE_SPAN - 1 + rim_width))
    need_f = jnp.where(need, 1.0, 0.0)
    upper = (
        lax.broadcasted_iota(jnp.int32, (events, events), 0)
        <= lax.broadcasted_iota(jnp.int32, (events, events), 1)
    )
    upper = jnp.where(upper, 1.0, 0.0).astype(bf16)
    pos = jnp.dot(need_f.astype(bf16), upper, preferred_element_type=f32)
    pos_s[0:blocks] = pos
    posm_s[0:blocks] = jnp.where(need, pos, 0.0)
    pad = (8, events)
    pos_s[blocks : blocks + 8] = jnp.zeros(pad, f32)
    posm_s[blocks : blocks + 8] = jnp.zeros(pad, f32)

    count = jnp.sum(need_f, axis=1, keepdims=True)
    units = jnp.floor((count + (UNIT - 1)) * (1.0 / UNIT))
    lower = (
        lax.broadcasted_iota(jnp.int32, (blocks, blocks), 0)
        >= lax.broadcasted_iota(jnp.int32, (blocks, blocks), 1)
    )
    ends = jnp.dot(
        jnp.where(lower, 1.0, 0.0).astype(bf16),
        jnp.broadcast_to(units, (blocks, LANES)).astype(bf16),
        preferred_element_type=f32,
    )
    lane = lax.broadcasted_iota(jnp.int32, (1, LANES), 1)

    def list_part(k, carry):
        at = k * LANES
        if not isinstance(k, int):
            at = pl.multiple_of(at, LANES)
        u = (lane + at).astype(f32)
        done = ends <= u
        blk_v[:, pl.ds(at, LANES)] = jnp.sum(
            jnp.where(done, 1.0, 0.0), axis=0, keepdims=True
        ).astype(jnp.int32)
        start = jnp.max(jnp.where(done, ends, 0.0), axis=0, keepdims=True)
        fst_v[:, pl.ds(at, LANES)] = (u - start) * float(UNIT)
        return carry

    if listed <= 16 * LANES:
        for k in range(listed // LANES):
            list_part(k, 0)
    else:
        lax.fori_loop(0, listed // LANES, list_part, 0)
    copies = [
        pltpu.make_async_copy(blk_v, blk_s, sems.at[0]),
        pltpu.make_async_copy(fst_v, fst_s, sems.at[1]),
    ]
    for copy in copies:
        copy.start()

    t_s[0:blocks] = times
    r_s[0:blocks] = rows
    c_s[0:blocks] = g_ref[:, 0, 2 * events : 3 * events]
    b_s[0:blocks] = g_ref[:, 0, 4 * events : 5 * events]
    producing = jnp.full_like(mag, prod_ref[0])
    sigma = jnp.full_like(mag, spread_ref[0])
    for k in range(1, nbin):
        hit = mag == float(k)
        producing = jnp.where(hit, prod_ref[k], producing)
        sigma = jnp.where(hit, spread_ref[k], sigma)
    norm = (omori_power - 1.0) * omori_offset ** (omori_power - 1.0) / (2.0 * math.pi)
    area = sigma * sigma
    l_s[0:blocks] = jnp.log(producing * norm / area) * LOG2E
    v_s[0:blocks] = (0.5 * cell_km * cell_km * LOG2E) / area
    t_s[blocks : blocks + 8] = jnp.broadcast_to(times[0:1, 0:1], pad)
    r_s[blocks : blocks + 8] = jnp.zeros(pad, f32)
    c_s[blocks : blocks + 8] = jnp.zeros(pad, f32)
    b_s[blocks : blocks + 8] = jnp.zeros(pad, f32)
    l_s[blocks : blocks + 8] = jnp.full(pad, -1e30, f32)
    v_s[blocks : blocks + 8] = jnp.zeros(pad, f32)
    x_s[...] = jnp.zeros_like(x_s)
    sel_s[...] = jnp.zeros_like(sel_s)
    dep_s[...] = jnp.zeros_like(dep_s)

    def part(ref, b, h):
        return ref[pl.ds(b, 1), :][:, h * LANES : (h + 1) * LANES]

    def source(b, back):
        return b if back == 0 else jnp.where(b >= back, b - back, blocks)

    def lane_sums(t_i, r_i, c_i, b, before):
        total = None
        for back in range(NB + 1):
            s = source(b, back)
            for h in range(halves):
                gap = (t_i - part(t_s, s, h)) + omori_offset
                dr = r_i - part(r_s, s, h)
                dc = c_i - part(c_s, s, h)
                expo = (part(l_s, s, h) - (omori_power * LOG2E) * jnp.log(gap)) - (
                    dr * dr + dc * dc
                ) * part(v_s, s, h)
                term = jnp.exp2(expo)
                if back == 0:
                    term = jnp.where(before(h), term, 0.0)
                total = term if total is None else total + term
        return jnp.sum(total, axis=1, keepdims=True)

    sub = lax.broadcasted_iota(jnp.int32, (UNIT, LANES), 0)
    lane_u = lax.broadcasted_iota(jnp.int32, (UNIT, LANES), 1)
    own_rows = jnp.concatenate(
        [t_s[pl.ds(own, 1), :], r_s[pl.ds(own, 1), :], c_s[pl.ds(own, 1), :], jnp.zeros((5, events), f32)]
    )
    own_cols = jnp.transpose(own_rows)
    for h in range(halves):
        found = jnp.zeros((UNIT, LANES), f32)
        for j in range(LANES // UNIT):
            at = h * LANES + j * UNIT
            cols = own_cols[at : at + UNIT]
            target = sub + j * UNIT

            def before(k, h=h, target=target):
                return lane_u + (k - h) * LANES < target

            trig = lane_sums(cols[:, 0:1], cols[:, 1:2], cols[:, 2:3], own, before)
            found = found + jnp.where(lane_u == target, trig, 0.0)
        found = jnp.sum(found, axis=0, keepdims=True)
        logint_ref[:, h * LANES : (h + 1) * LANES] = jnp.log(part(b_s, own, h) + found)

    for copy in copies:
        copy.wait()
    total_units = (listed - 1) - (fst_s[0, listed - 1] * (1.0 / UNIT)).astype(jnp.int32)

    rank = sub.astype(f32) + 1.0
    slots = STEP * UNIT
    m_row = (lax.broadcasted_iota(jnp.int32, (slots, LANES), 1) % LATITUDE_SPAN).astype(f32)
    lane_s = lax.broadcasted_iota(jnp.int32, (slots, LANES), 1)
    m_hi = (lane_s // LATITUDE_SPAN).astype(f32)
    lane_f = lane_s.astype(f32)

    def flush():
        x_s[8 : 8 + M_ROWS] += lax.dot_general(
            a_buf[...], b_buf[...], (((0,), (0,)), ((), ())), preferred_element_type=f32
        )

    def step(i, carry):
        r_i, c_i, b_i, trig = dep_s[0], dep_s[1], dep_s[2], dep_s[3]
        share = jnp.where(b_i > 0.0, b_i / (b_i + trig), 0.0)
        share = share.astype(bf16).astype(f32)
        hi = jnp.floor(c_i * (1.0 / LO_COLS))
        lo = c_i - hi * LO_COLS
        d = m_row - (r_i - first_row)
        d2 = d * d
        w = jnp.exp2(d2 * (-LOG2E / (2.0 * smooth_sigma**2))) * (share * (1.0 / WEIGHT_SUM))
        w = jnp.where(d2 < (rim_width + 0.5) ** 2, w, 0.0)
        slot = pl.multiple_of(lax.rem(i + (BATCH // slots - 2), BATCH // slots) * slots, slots)
        for h in range(M_ROWS // LANES):
            a = jnp.where(m_hi == hi - float(h * (LANES // LATITUDE_SPAN)), w, 0.0)
            a_buf[pl.ds(slot, slots), h * LANES : (h + 1) * LANES] = a.astype(bf16)
        for h in range(LO_COLS // LANES):
            b = jnp.where(lane_f == lo - float(h * LANES), 1.0, 0.0)
            b_buf[pl.ds(slot, slots), h * LANES : (h + 1) * LANES] = b.astype(bf16)
        for j in range(STEP):
            u = jnp.maximum((i - 1) * STEP + j, 0)
            b = blk_s[0, u]
            order = rank + fst_s[0, u]
            at = slice(j * UNIT, (j + 1) * UNIT)
            t_i, r_i, c_i = sel_s[0, at], sel_s[1, at], sel_s[2, at]
            trig = lane_sums(t_i, r_i, c_i, b, lambda h: part(pos_s, b, h) < order)
            dep_s[0, at] = r_i
            dep_s[1, at] = c_i
            dep_s[2, at] = sel_s[3, at]
            dep_s[3, at] = jnp.broadcast_to(trig, (UNIT, LANES))
        for j in range(STEP):
            u = i * STEP + j
            b = blk_s[0, u]
            order = rank + fst_s[0, u]
            picks = [part(posm_s, b, h) == order for h in range(halves)]
            for k, ref in enumerate((t_s, r_s, c_s, b_s)):
                value = None
                for h in range(halves):
                    piece = jnp.where(picks[h], part(ref, b, h), 0.0)
                    value = piece if value is None else value + piece
                value = jnp.sum(value, axis=1, keepdims=True)
                sel_s[k, j * UNIT : (j + 1) * UNIT] = jnp.broadcast_to(value, (UNIT, LANES))

        @pl.when(slot == BATCH - slots)
        def _():
            flush()
            a_buf[...] = jnp.zeros_like(a_buf)

        return carry

    a_buf[...] = jnp.zeros_like(a_buf)
    b_buf[...] = jnp.zeros_like(b_buf)
    lax.fori_loop(0, (total_units + (STEP - 1)) // STEP + 2, step, 0)
    flush()

    span = LATITUDE_SPAN
    wide = LO_COLS // LANES
    tall = 16
    lane_t = lax.broadcasted_iota(jnp.int32, (tall, LANES), 1)
    for m in range(0, M_ROWS, tall):
        def tile(shift, h):
            return x_s[8 + m + shift : 8 + m + shift + tall, h * LANES : (h + 1) * LANES]

        mids = [tile(0, h) for h in range(wide)]
        lefts = [tile(-span, wide - 1)] + mids[:-1]
        rights = mids[1:] + [tile(span, 0)]
        for h in range(wide):
            acc = mids[h] * (WEIGHTS[rim_width] / WEIGHT_SUM)
            for b in range(1, rim_width + 1):
                from_left = pltpu.roll(jnp.where(lane_t >= LANES - b, lefts[h], mids[h]), b, 1)
                from_right = pltpu.roll(jnp.where(lane_t < b, rights[h], mids[h]), LANES - b, 1)
                acc = acc + (from_left + from_right) * (WEIGHTS[rim_width + b] / WEIGHT_SUM)
            for q in range(tall // span):
                at = (m // span + q) * LO_COLS + h * LANES
                dens_ref[:, at : at + LANES] = acc[q * span : (q + 1) * span]


def body(times, cell_row, cell_col, magnitude, base_rate, productivity, spread):
    events = times.shape[0]
    blocks = lax.axis_size(AXES)
    f32 = jnp.float32
    rows = [x.reshape(1, events) for x in (times, cell_row, cell_col, magnitude, base_rate)]
    vmem = pl.BlockSpec(memory_space=pltpu.VMEM)
    smem = pl.BlockSpec(memory_space=pltpu.SMEM)
    spread_out = pl.pallas_call(
        spread_kernel,
        out_shape=jax.ShapeDtypeStruct((blocks, 1, 5 * events), f32),
        in_specs=[vmem] * 5,
        out_specs=vmem,
        compiler_params=pltpu.CompilerParams(vmem_limit_bytes=16 * MIB),
    )(*rows)
    gathered = lax.all_to_all(spread_out, AXES, 0, 0, tiled=True)
    listed = blocks * events // UNIT + LANES
    field = pltpu.VMEM((blocks + 8, events), f32)
    log_intensity, density = pl.pallas_call(
        kernel,
        out_shape=(
            jax.ShapeDtypeStruct((1, events), f32),
            jax.ShapeDtypeStruct((LATITUDE_SPAN, COLS), f32),
        ),
        in_specs=[vmem, smem, smem],
        out_specs=(vmem, vmem),
        scratch_shapes=[field] * 8
        + [
            pltpu.VMEM((1, listed), jnp.int32),
            pltpu.VMEM((1, listed), f32),
            pltpu.SMEM((1, listed), jnp.int32),
            pltpu.SMEM((1, listed), f32),
            pltpu.VMEM((4, STEP * UNIT, LANES), f32),
            pltpu.VMEM((4, STEP * UNIT, LANES), f32),
            pltpu.VMEM((BATCH, M_ROWS), jnp.bfloat16),
            pltpu.VMEM((BATCH, LO_COLS), jnp.bfloat16),
            pltpu.VMEM((M_ROWS + 16, LO_COLS), f32),
            pltpu.SemaphoreType.DMA((2,)),
        ],
        compiler_params=pltpu.CompilerParams(vmem_limit_bytes=32 * MIB),
    )(gathered, productivity, spread)
    return (log_intensity.reshape(events), density)


def solution(mesh):
    in_specs = (P(AXES), P(AXES), P(AXES), P(AXES), P(AXES), P(), P())
    out_specs = (P(AXES), P(AXES, None))
    return jax.shard_map(body, mesh=mesh, in_specs=in_specs, out_specs=out_specs, check_vma=False)
```

time: 29.1 us -> 26.4 us (0.907)
  local copies, waits for them, and re-layouts: 4.12 us -> 0.71 us
  Pallas kernels: 7.81 us -> 8.47 us
    unnamed x12 -> x14, local copies, waits for them, and re-layouts: 4.03 us -> 0.71 us
    pallas_call x1, Pallas kernels: 7.81 us -> 8.42 us  [body(): pl.pallas_call(kernel, out_shape=(jax.ShapeDtypeStruct((1, events), f32),...]
where the time goes in v2:
time: 26.4 us; the launch traced here: 26.1 us
  blocking collectives  16.2 us (61%)
  Pallas kernels  8.47 us (32%)
  local copies, waits for them, and re-layouts  0.71 us (3%)
  between operations  0.69 us (3%)
    all_to_all x1, blocking collectives, body(): gathered = lax.all_to_all(spread_out, AXES, 0, 0, tiled=True)  16.2 us
    pallas_call x1, Pallas kernels, body(): pl.pallas_call(kernel, out_shape=(jax.ShapeDtypeStruct((1, events), f32),...  8.42 us
    unnamed x14, local copies, waits for them, and re-layouts  0.71 us

profile of v2, /device:TPU:0, one launch (start us, length us, event | category | flops | bytes accessed | tf_op | source)
XLA Modules:
  0.0 26.1 jit_solution(8973866794700907885)
XLA Ops:
  0.6 0.0 copy-start.3
  0.6 0.0 copy-start.4
  0.7 0.0 copy-start.1
  0.7 0.0 copy-start.2
  0.7 0.0 copy-start
  0.7 0.6 %copy-done.3 = s32[256]{0:T(256)S(1)} copy-done((s32[256]{0:T(256)S(1)}, s32[256]{0:T(256)}, u32[]{:S(2)}) %copy-start.3) | copy-done | bytes 1048
  1.3 0.0 copy-done.4
  1.3 0.0 copy-done.1
  1.3 0.0 copy-done.2
  1.4 0.0 copy-done
  1.4 0.0 copy-start.5
  1.4 0.0 copy-start.6
  1.4 16.2 %all_to_all.5.g_ref = f32[32,1,1280]{2,1,0:T(1,128)S(1)} all-to-all(f32[32,1,1280]{2,1,0:T(1,128)S(1)} %shard_map.86), channel_id=1, replica_groups=mesh['tm'=16,'grid'=2] {'tm','grid'}, dimensions={0} | all-to-all | bytes 327680 | tf_op jit(solution)/shard_map/all_to_all | solution.py:283
  17.7 0.0 copy-done.5
  17.7 0.0 copy-done.6
  17.7 8.4 %shard_map.87 = (f32[1,256]{1,0:T(1,128)}, f32[4,16384]{1,0:T(4,128)}) custom-call(f32[32,1,1280]{2,1,0:T(1,128)S(1)} %all_to_all.5.g_ref, f32[8]{0:T(128)S(1)} %copy-done.5, f32[8]{0:T(128)S(1)} %copy-done.6), custom_call_target="tpu_custom_call" | custom-call | tf_op jit(solution)/shard_map/pallas_call | solution.py:286
  (1 shorter events, 0.0 us)
Async XLA Ops:
  0.6 0.7 %copy-start.3 = (s32[256]{0:T(256)S(1)}, s32[256]{0:T(256)}, u32[]{:S(2)}) copy-start(s32[256]{0:T(256)} %param.10) | copy-start | bytes 3076
  0.6 0.7 %copy-start.4 = (f32[256]{0:T(256)S(1)}, f32[256]{0:T(256)}, u32[]{:S(2)}) copy-start(f32[256]{0:T(256)} %param.11) | copy-start | bytes 3076
  0.7 0.7 %copy-start.1 = (s32[256]{0:T(256)S(1)}, s32[256]{0:T(256)}, u32[]{:S(2)}) copy-start(s32[256]{0:T(256)} %param.8) | copy-start | bytes 3076
  0.7 0.7 %copy-start.2 = (s32[256]{0:T(256)S(1)}, s32[256]{0:T(256)}, u32[]{:S(2)}) copy-start(s32[256]{0:T(256)} %param.9) | copy-start | bytes 3076
  0.7 0.7 %copy-start = (f32[256]{0:T(256)S(1)}, f32[256]{0:T(256)}, u32[]{:S(2)}) copy-start(f32[256]{0:T(256)} %param.7) | copy-start | bytes 3076
  1.4 16.3 %copy-start.5 = (f32[8]{0:T(128)S(1)}, f32[8]{0:T(128)}, u32[]{:S(2)}) copy-start(f32[8]{0:T(128)} %prod_ref.1) | copy-start | bytes 100
  1.4 16.3 %copy-start.6 = (f32[8]{0:T(128)S(1)}, f32[8]{0:T(128)}, u32[]{:S(2)}) copy-start(f32[8]{0:T(128)} %spread_ref.1) | copy-start | bytes 100

commit v3 on v2

v3 whole, which is shorter than its diff:
```python
import math

import jax
import jax.numpy as jnp
from jax import lax
from jax.experimental import pallas as pl
from jax.experimental.pallas import tpu as pltpu
from jax.sharding import PartitionSpec as P

NB = 2
LATITUDE_SPAN = 4
COLS = 16384

omori_power = 1.2
omori_offset = 0.5
cell_km = 0.1
smooth_sigma = 1.5
rim_width = 3

AXES = ("tm", "grid")
LANES = 128
UNIT = 8
STEP = 8
BATCH = 256
LO_COLS = 256
M_ROWS = LATITUDE_SPAN * (COLS // LO_COLS)
LOG2E = math.log2(math.e)
WEIGHTS = [math.exp(-(b * b) / (2.0 * smooth_sigma**2)) for b in range(-rim_width, rim_width + 1)]
WEIGHT_SUM = sum(WEIGHTS)
MIB = 1 << 20
FT = jnp.bfloat16


def spread_kernel(t_ref, r_ref, c_ref, m_ref, b_ref, prod_ref, spread_ref, out_ref, l_ref, v_ref):
    norm = (omori_power - 1.0) * omori_offset ** (omori_power - 1.0) / (2.0 * math.pi)
    area = spread_ref[...] * spread_ref[...]
    l_ref[...] = jnp.log(prod_ref[...] * norm / area) * LOG2E
    v_ref[...] = (0.5 * cell_km * cell_km * LOG2E) / area
    events = t_ref.shape[1]
    shape = (out_ref.shape[0], 1, events)
    for k, ref in enumerate([t_ref, r_ref, c_ref, m_ref, b_ref]):
        row = ref[...].astype(jnp.float32)
        out_ref[:, :, k * events : (k + 1) * events] = jnp.broadcast_to(row[None], shape)


def kernel(g_ref, lof_ref, vof_ref, logint_ref, dens_ref,
           t_s, l_s, v_s, pos_s, posm_s, own_s,
           blk_v, fst_v, blk_s, fst_s, sel_s, dep_s, a_buf, b_buf, x_s, sems):
    f32 = jnp.float32
    bf16 = jnp.bfloat16
    i32 = jnp.int32
    blocks = g_ref.shape[0]
    events = g_ref.shape[2] // 5
    halves = events // LANES
    nbin = lof_ref.shape[1]
    listed = blk_v.shape[1]
    tall = 8
    own = lax.axis_index("tm") * lax.axis_size("grid") + lax.axis_index("grid")
    first_row = (own * LATITUDE_SPAN).astype(f32)

    l_of = lof_ref[...]
    v_of = vof_ref[...]

    def fields(k, carry):
        at = pl.ds(pl.multiple_of(k * tall, tall), tall)
        t_s[at] = g_ref[at, 0, 0:events]
        rows = g_ref[at, 0, events : 2 * events]
        mag = g_ref[at, 0, 3 * events : 4 * events]
        need = (rows >= first_row - rim_width) & (
            rows <= first_row + (LATITUDE_SPAN - 1 + rim_width)
        )
        posm_s[at] = jnp.where(need, 1.0, 0.0)
        l_j = jnp.broadcast_to(l_of[:, 0:1], mag.shape)
        v_j = jnp.broadcast_to(v_of[:, 0:1], mag.shape)
        for n in range(1, nbin):
            hit = mag == float(n)
            l_j = jnp.where(hit, l_of[:, n : n + 1], l_j)
            v_j = jnp.where(hit, v_of[:, n : n + 1], v_j)
        l_s[at] = l_j
        v_s[at] = v_j
        return carry

    lax.fori_loop(0, blocks // tall, fields, 0)
    pad = (tall, events)
    t_s[blocks : blocks + tall] = jnp.broadcast_to(g_ref[0:1, 0, 0:1], pad)
    l_s[blocks : blocks + tall] = jnp.full(pad, -1e30, f32)

    need_f = posm_s[...]
    upper = lax.broadcasted_iota(i32, (events, events), 0) <= lax.broadcasted_iota(
        i32, (events, events), 1
    )
    upper = jnp.where(upper, 1.0, 0.0).astype(bf16)
    pos = jnp.dot(need_f.astype(bf16), upper, preferred_element_type=f32)
    pos_s[...] = pos
    posm_s[...] = need_f * pos

    count = jnp.sum(need_f, axis=1, keepdims=True)
    units = jnp.floor((count + (UNIT - 1)) * (1.0 / UNIT))
    lower = lax.broadcasted_iota(i32, (blocks, blocks), 0) >= lax.broadcasted_iota(
        i32, (blocks, blocks), 1
    )
    ends = jnp.dot(
        jnp.where(lower, 1.0, 0.0).astype(bf16),
        jnp.broadcast_to(units, (blocks, LANES)).astype(bf16),
        preferred_element_type=f32,
    )
    lane = lax.broadcasted_iota(i32, (1, LANES), 1)
    beyond = 1e6

    def list_part(k, carry):
        at = k * LANES
        if not isinstance(k, int):
            at = pl.multiple_of(at, LANES)
        u = (lane + at).astype(f32)
        done = ends <= u
        blk = jnp.sum(jnp.where(done, 1.0, 0.0), axis=0, keepdims=True)
        start = jnp.max(jnp.where(done, ends, 0.0), axis=0, keepdims=True)
        last = float(blocks - 1)
        blk_v[:, pl.ds(at, LANES)] = jnp.minimum(blk, last).astype(i32)
        fst_v[:, pl.ds(at, LANES)] = (u - start) * float(UNIT) + jnp.where(blk > last, beyond, 0.0)
        return carry

    if listed <= 16 * LANES:
        for k in range(listed // LANES):
            list_part(k, 0)
    else:
        lax.fori_loop(0, listed // LANES, list_part, 0)
    copies = [
        pltpu.make_async_copy(blk_v, blk_s, sems.at[0]),
        pltpu.make_async_copy(fst_v, fst_s, sems.at[1]),
    ]
    for copy in copies:
        copy.start()

    x_s[...] = jnp.zeros_like(x_s)
    dep_s[...] = jnp.zeros_like(dep_s)
    a_buf[...] = jnp.zeros_like(a_buf)
    b_buf[...] = jnp.zeros_like(b_buf)

    def part(ref, b, h):
        return ref[pl.ds(b, 1), :][:, h * LANES : (h + 1) * LANES]

    def given(field, b, h):
        at = field * events + h * LANES
        return g_ref[b, 0:1, at : at + LANES]

    def lane_sums(t_i, r_i, c_i, b, before):
        total = None
        for back in range(NB + 1):
            near = b if back == 0 else jnp.maximum(b - back, 0)
            s = b if back == 0 else jnp.where(b >= back, b - back, blocks)
            for h in range(halves):
                gap = (t_i - part(t_s, s, h)) + omori_offset
                dr = r_i - given(1, near, h)
                dc = c_i - given(2, near, h)
                expo = (part(l_s, s, h) - (omori_power * LOG2E) * jnp.log(gap)) - (
                    dr * dr + dc * dc
                ) * part(v_s, near, h)
                term = jnp.exp2(expo)
                if back == 0:
                    term = jnp.where(before(h), term, 0.0)
                total = term if total is None else total + term
        return jnp.sum(total, axis=1, keepdims=True)

    sub_f = lax.broadcasted_iota(i32, (UNIT, LANES), 0).astype(f32)
    lane_f = lax.broadcasted_iota(i32, (UNIT, LANES), 1).astype(f32)
    own_rows = jnp.concatenate(
        [g_ref[own, 0:1, k * events : (k + 1) * events] for k in range(3)]
        + [jnp.zeros((5, events), f32)]
    )
    own_cols = jnp.transpose(own_rows)
    for k in range(3):
        own_s[k] = jnp.broadcast_to(own_cols[:, k : k + 1], (events, LANES))

    def own_step(k, found):
        for j in range(STEP):
            at = k * (STEP * UNIT) + j * UNIT
            target = sub_f + at.astype(f32)
            t_i, r_i, c_i = (own_s[n, pl.ds(pl.multiple_of(at, UNIT), UNIT)] for n in range(3))
            trig = lane_sums(t_i, r_i, c_i, own, lambda h: lane_f + h * LANES < target)
            found = tuple(
                found[h] + jnp.where(lane_f + h * LANES == target, trig, 0.0) for h in range(halves)
            )
        return found

    found = lax.fori_loop(
        0, events // (STEP * UNIT), own_step, tuple(jnp.zeros((UNIT, LANES), f32) for _ in range(halves))
    )
    for h in range(halves):
        trig = jnp.sum(found[h], axis=0, keepdims=True)
        logint_ref[:, h * LANES : (h + 1) * LANES] = jnp.log(given(4, own, h) + trig)

    for copy in copies:
        copy.wait()
    total_units = (listed - 1) - ((fst_s[0, listed - 1] - beyond) * (1.0 / UNIT)).astype(i32)

    rank = sub_f + 1.0
    slots = STEP * UNIT
    steps = BATCH // slots
    lane_s = lax.broadcasted_iota(i32, (slots, LANES), 1)
    m_row = (lane_s % LATITUDE_SPAN).astype(f32)
    col_blocks = M_ROWS // LATITUDE_SPAN
    m_hi = []
    for h in range(M_ROWS // LANES):
        m = lane_s + h * LANES
        m_hi.append((m // LATITUDE_SPAN % 2 * (col_blocks // 2) + m // (2 * LATITUDE_SPAN)).astype(FT))
    l_lo = [(lane_s + h * LANES).astype(FT) for h in range(LO_COLS // LANES)]
    zero, one = jnp.zeros((), FT), jnp.ones((), FT)

    def flush(size):
        x_s[8 : 8 + M_ROWS] += lax.dot_general(
            a_buf[0:size], b_buf[0:size], (((0,), (0,)), ((), ())), preferred_element_type=f32
        )

    def factors(slot):
        r_i, c_i, b_i, trig = dep_s[0], dep_s[1], dep_s[2], dep_s[3]
        share = jnp.where(b_i > 0.0, b_i / (b_i + trig), 0.0)
        share = share.astype(bf16).astype(f32)
        hi = jnp.floor(c_i * (1.0 / LO_COLS))
        lo = (c_i - hi * LO_COLS).astype(FT)
        hi = hi.astype(FT)
        d = m_row - (r_i - first_row)
        d2 = d * d
        w = jnp.exp2(d2 * (-LOG2E / (2.0 * smooth_sigma**2))) * share
        w = jnp.where(d2 < (rim_width + 0.5) ** 2, w, 0.0).astype(FT)
        at = pl.ds(pl.multiple_of(slot * slots, slots), slots)
        for h in range(M_ROWS // LANES):
            a_buf[at, h * LANES : (h + 1) * LANES] = jnp.where(m_hi[h] == hi, w, zero).astype(bf16)
        for h in range(LO_COLS // LANES):
            b_buf[at, h * LANES : (h + 1) * LANES] = jnp.where(l_lo[h] == lo, one, zero).astype(bf16)

    def unit_triggers(i):
        for j in range(STEP):
            u = i * STEP + j
            b = blk_s[0, u]
            order = rank + fst_s[0, u]
            at = slice(j * UNIT, (j + 1) * UNIT)
            t_i, r_i, c_i = sel_s[0, at], sel_s[1, at], sel_s[2, at]
            trig = lane_sums(t_i, r_i, c_i, b, lambda h: part(pos_s, b, h) < order)
            dep_s[0, at] = r_i
            dep_s[1, at] = c_i
            dep_s[2, at] = sel_s[3, at]
            dep_s[3, at] = jnp.broadcast_to(trig, (UNIT, LANES))

    def pick_events(i):
        for j in range(STEP):
            u = i * STEP + j
            b = blk_s[0, u]
            order = rank + fst_s[0, u]
            picks = [part(posm_s, b, h) == order for h in range(halves)]
            for k, field in enumerate((0, 1, 2, 4)):
                value = None
                for h in range(halves):
                    piece = jnp.where(picks[h], given(field, b, h), 0.0)
                    value = piece if value is None else value + piece
                value = jnp.sum(value, axis=1, keepdims=True)
                sel_s[k, j * UNIT : (j + 1) * UNIT] = jnp.broadcast_to(value, (UNIT, LANES))

    total_steps = (total_units + (STEP - 1)) // STEP
    pick_events(0)

    def batch(q, carry):
        @pl.when(q > 0)
        def _():
            flush(BATCH)
            a_buf[...] = jnp.zeros_like(a_buf)

        def step(k, carry):
            i = q * steps + k
            factors(k)
            unit_triggers(i)
            pick_events(i + 1)
            return carry

        return lax.fori_loop(0, jnp.minimum(total_steps - q * steps, steps), step, 0)

    batches = (total_steps + (steps - 1)) // steps
    lax.fori_loop(0, batches, batch, 0)
    factors(total_steps - jnp.maximum(batches - 1, 0) * steps)
    flush(BATCH + slots)

    span = LATITUDE_SPAN
    wide = LO_COLS // LANES
    middle = (col_blocks // 2) * LO_COLS
    zeros = jnp.zeros((span, LO_COLS), f32)
    x_s[0:8] = jnp.concatenate([zeros, x_s[M_ROWS : M_ROWS + span]])
    x_s[8 + M_ROWS : 16 + M_ROWS] = jnp.concatenate([x_s[8 + span : 16], zeros])
    lane_t = lax.broadcasted_iota(i32, (8, LANES), 1)
    per = 4

    def columns(g, carry):
        for p in range(per):
            m = g * (8 * per) + 8 * p

            def tile(shift, h):
                return x_s[pl.ds(pl.multiple_of(m + 8 + shift, 8), 8), h * LANES : (h + 1) * LANES]

            mids = [tile(0, h) for h in range(wide)]
            lefts = [tile(-8, wide - 1)] + mids[:-1]
            rights = mids[1:] + [tile(8, 0)]
            for h in range(wide):
                acc = mids[h] * (WEIGHTS[rim_width] / WEIGHT_SUM**2)
                for b in range(1, rim_width + 1):
                    from_left = pltpu.roll(jnp.where(lane_t >= LANES - b, lefts[h], mids[h]), b, 1)
                    from_right = pltpu.roll(jnp.where(lane_t < b, rights[h], mids[h]), LANES - b, 1)
                    acc = acc + (from_left + from_right) * (WEIGHTS[rim_width + b] / WEIGHT_SUM**2)
                at = (g * per + p) * LO_COLS + h * LANES
                for half in range(2):
                    place = pl.ds(pl.multiple_of(at + half * middle, LANES), LANES)
                    dens_ref[:, place] = acc[half * span : (half + 1) * span]
        return carry

    lax.fori_loop(0, M_ROWS // (8 * per), columns, 0)


def body(times, cell_row, cell_col, magnitude, base_rate, productivity, spread):
    events = times.shape[0]
    blocks = lax.axis_size(AXES)
    f32 = jnp.float32
    rows = [x.reshape(1, events) for x in (times, cell_row, cell_col, magnitude, base_rate)]
    vmem = pl.BlockSpec(memory_space=pltpu.VMEM)
    rows += [x.reshape(1, -1) for x in (productivity, spread)]
    table = jax.ShapeDtypeStruct((1, productivity.shape[0]), f32)
    spread_out, l_table, v_table = pl.pallas_call(
        spread_kernel,
        out_shape=(jax.ShapeDtypeStruct((blocks, 1, 5 * events), f32), table, table),
        in_specs=[vmem] * 7,
        out_specs=(vmem, vmem, vmem),
        compiler_params=pltpu.CompilerParams(vmem_limit_bytes=16 * MIB),
    )(*rows)
    gathered = lax.all_to_all(spread_out, AXES, 0, 0, tiled=True)
    listed = blocks * events // UNIT + LANES
    padded = pltpu.VMEM((blocks + 8, events), f32)
    field = pltpu.VMEM((blocks, events), f32)
    log_intensity, density = pl.pallas_call(
        kernel,
        out_shape=(
            jax.ShapeDtypeStruct((1, events), f32),
            jax.ShapeDtypeStruct((LATITUDE_SPAN, COLS), f32),
        ),
        in_specs=[vmem, vmem, vmem],
        out_specs=(vmem, vmem),
        scratch_shapes=[
            padded, padded, field, field, field,
            pltpu.VMEM((3, events, LANES), f32),
            pltpu.VMEM((1, listed), jnp.int32),
            pltpu.VMEM((1, listed), f32),
            pltpu.SMEM((1, listed), jnp.int32),
            pltpu.SMEM((1, listed), f32),
            pltpu.VMEM((4, STEP * UNIT, LANES), f32),
            pltpu.VMEM((4, STEP * UNIT, LANES), f32),
            pltpu.VMEM((BATCH + STEP * UNIT, M_ROWS), jnp.bfloat16),
            pltpu.VMEM((BATCH + STEP * UNIT, LO_COLS), jnp.bfloat16),
            pltpu.VMEM((M_ROWS + 16, LO_COLS), f32),
            pltpu.SemaphoreType.DMA((2,)),
        ],
        compiler_params=pltpu.CompilerParams(vmem_limit_bytes=32 * MIB),
    )(gathered, l_table, v_table)
    return (log_intensity.reshape(events), density)


def solution(mesh):
    in_specs = (P(AXES), P(AXES), P(AXES), P(AXES), P(AXES), P(), P())
    out_specs = (P(AXES), P(AXES, None))
    return jax.shard_map(body, mesh=mesh, in_specs=in_specs, out_specs=out_specs, check_vma=False)
```

time: 26.4 us -> 24.4 us (0.924)
  Pallas kernels: 8.47 us -> 6.58 us
    pallas_call x1, Pallas kernels: 8.42 us -> 6.53 us  [body(): pl.pallas_call(kernel, out_shape=(jax.ShapeDtypeStruct((1, events), f32),...]
where the time goes in v3:
time: 24.4 us; the launch traced here: 24.2 us
  blocking collectives  16.2 us (66%)
  Pallas kernels  6.58 us (27%)
  local copies, waits for them, and re-layouts  0.7 us (3%)
  between operations  0.7 us (3%)
    all_to_all x1, blocking collectives, body(): gathered = lax.all_to_all(spread_out, AXES, 0, 0, tiled=True)  16.2 us
    pallas_call x1, Pallas kernels, body(): pl.pallas_call(kernel, out_shape=(jax.ShapeDtypeStruct((1, events), f32),...  6.53 us
    unnamed x14, local copies, waits for them, and re-layouts  0.7 us

profile of v3, /device:TPU:0, one launch (start us, length us, event | category | flops | bytes accessed | tf_op | source)
XLA Modules:
  0.0 24.2 jit_solution(18303948545378520332)
XLA Ops:
  0.6 0.0 copy-start.6
  0.6 0.0 copy-start.3
  0.7 0.0 copy-start.4
  0.7 0.0 copy-start.1
  0.7 0.0 copy-start.2
  0.7 0.0 copy-start
  0.7 0.0 copy-start.5
  0.7 0.6 %copy-done.6 = f32[8]{0:T(128)S(1)} copy-done((f32[8]{0:T(128)S(1)}, f32[8]{0:T(128)}, u32[]{:S(2)}) %copy-start.6) | copy-done | bytes 56
  1.3 0.0 copy-done.3
  1.3 0.0 copy-done.4
  1.3 0.0 copy-done.1
  1.4 0.0 copy-done.2
  1.4 0.0 copy-done
  1.4 0.0 copy-done.5
  1.4 16.2 %all_to_all.5.g_ref = f32[32,1,1280]{2,1,0:T(1,128)S(1)} all-to-all(f32[32,1,1280]{2,1,0:T(1,128)S(1)} %get-tuple-element.7), channel_id=1, replica_groups=mesh['tm'=16,'grid'=2] {'tm','grid'}, dimensions={0} | all-to-all | bytes 327680 | tf_op jit(solution)/shard_map/all_to_all | solution.py:331
  17.7 6.5 %shard_map.87 = (f32[1,256]{1,0:T(1,128)}, f32[4,16384]{1,0:T(4,128)}) custom-call(f32[32,1,1280]{2,1,0:T(1,128)S(1)} %all_to_all.5.g_ref, f32[1,8]{1,0:T(1,128)S(1)} %get-tuple-element.8.lof_ref, f32[1,8]{1,0:T(1,128)S(1)} %get-tuple-element.9.vof_ref), custom_call_target="tpu_custom_call" | custom-call | tf_op jit(solution)/shard_map/pallas_call | solution.py:335
  (1 shorter events, 0.0 us)
Async XLA Ops:
  0.6 0.7 %copy-start.6 = (f32[8]{0:T(128)S(1)}, f32[8]{0:T(128)}, u32[]{:S(2)}) copy-start(f32[8]{0:T(128)} %param.13) | copy-start | bytes 100
  0.6 0.7 %copy-start.3 = (s32[256]{0:T(256)S(1)}, s32[256]{0:T(256)}, u32[]{:S(2)}) copy-start(s32[256]{0:T(256)} %param.10) | copy-start | bytes 3076
  0.7 0.7 %copy-start.4 = (f32[256]{0:T(256)S(1)}, f32[256]{0:T(256)}, u32[]{:S(2)}) copy-start(f32[256]{0:T(256)} %param.11) | copy-start | bytes 3076
  0.7 0.7 %copy-start.1 = (s32[256]{0:T(256)S(1)}, s32[256]{0:T(256)}, u32[]{:S(2)}) copy-start(s32[256]{0:T(256)} %param.8) | copy-start | bytes 3076
  0.7 0.7 %copy-start.2 = (s32[256]{0:T(256)S(1)}, s32[256]{0:T(256)}, u32[]{:S(2)}) copy-start(s32[256]{0:T(256)} %param.9) | copy-start | bytes 3076
  0.7 0.7 %copy-start = (f32[256]{0:T(256)S(1)}, f32[256]{0:T(256)}, u32[]{:S(2)}) copy-start(f32[256]{0:T(256)} %param.7) | copy-start | bytes 3076
  0.7 0.7 %copy-start.5 = (f32[8]{0:T(128)S(1)}, f32[8]{0:T(128)}, u32[]{:S(2)}) copy-start(f32[8]{0:T(128)} %param.12) | copy-start | bytes 100

commit v4 on v3

--- a/solution.py
+++ b/solution.py
@@ -20,14 +20,18 @@
 AXES = ("tm", "grid")
 LANES = 128
 UNIT = 8
-STEP = 8
-BATCH = 256
+STEP = 16
+OWN_STEP = 16
+BATCH = 512
 LO_COLS = 256
 M_ROWS = LATITUDE_SPAN * (COLS // LO_COLS)
 LOG2E = math.log2(math.e)
 WEIGHTS = [math.exp(-(b * b) / (2.0 * smooth_sigma**2)) for b in range(-rim_width, rim_width + 1)]
 WEIGHT_SUM = sum(WEIGHTS)
 MIB = 1 << 20
+PER = 32
+FIELDS = 8
+T, R, C, L, V, B, RANK, PICK = range(FIELDS)
 FT = jnp.bfloat16
 
 
@@ -44,8 +48,7 @@
 
 
 def kernel(g_ref, lof_ref, vof_ref, logint_ref, dens_ref,
-           t_s, l_s, v_s, pos_s, posm_s, own_s,
-           blk_v, fst_v, blk_s, fst_s, sel_s, dep_s, a_buf, b_buf, x_s, sems):
+           all_s, own_s, blk_v, fst_v, blk_s, fst_s, sel_s, dep_s, a_buf, b_buf, x_s, sems):
     f32 = jnp.float32
     bf16 = jnp.bfloat16
     i32 = jnp.int32
@@ -63,36 +66,40 @@
 
     def fields(k, carry):
         at = pl.ds(pl.multiple_of(k * tall, tall), tall)
-        t_s[at] = g_ref[at, 0, 0:events]
+        times = g_ref[at, 0, 0:events]
         rows = g_ref[at, 0, events : 2 * events]
+        cols = g_ref[at, 0, 2 * events : 3 * events]
+        base = g_ref[at, 0, 4 * events : 5 * events]
         mag = g_ref[at, 0, 3 * events : 4 * events]
         need = (rows >= first_row - rim_width) & (
             rows <= first_row + (LATITUDE_SPAN - 1 + rim_width)
         )
-        posm_s[at] = jnp.where(need, 1.0, 0.0)
         l_j = jnp.broadcast_to(l_of[:, 0:1], mag.shape)
         v_j = jnp.broadcast_to(v_of[:, 0:1], mag.shape)
         for n in range(1, nbin):
             hit = mag == float(n)
             l_j = jnp.where(hit, l_of[:, n : n + 1], l_j)
             v_j = jnp.where(hit, v_of[:, n : n + 1], v_j)
-        l_s[at] = l_j
-        v_s[at] = v_j
+        need_f = jnp.where(need, 1.0, 0.0)
+        for f, value in ((T, times), (R, rows), (C, cols), (L, l_j), (V, v_j), (B, base), (PICK, need_f)):
+            all_s[f, at] = value
         return carry
 
     lax.fori_loop(0, blocks // tall, fields, 0)
     pad = (tall, events)
-    t_s[blocks : blocks + tall] = jnp.broadcast_to(g_ref[0:1, 0, 0:1], pad)
-    l_s[blocks : blocks + tall] = jnp.full(pad, -1e30, f32)
-
-    need_f = posm_s[...]
+    start = jnp.broadcast_to(g_ref[0:1, 0, 0:1], pad)
+    zeros = jnp.zeros(pad, f32)
+    for f, value in ((T, start), (R, zeros), (C, zeros), (L, jnp.full(pad, -1e30, f32)), (V, zeros)):
+        all_s[f, blocks : blocks + tall] = value
+
+    need_f = all_s[PICK, 0:blocks]
     upper = lax.broadcasted_iota(i32, (events, events), 0) <= lax.broadcasted_iota(
         i32, (events, events), 1
     )
     upper = jnp.where(upper, 1.0, 0.0).astype(bf16)
     pos = jnp.dot(need_f.astype(bf16), upper, preferred_element_type=f32)
-    pos_s[...] = pos
-    posm_s[...] = need_f * pos
+    all_s[RANK, 0:blocks] = pos
+    all_s[PICK, 0:blocks] = need_f * pos
 
     count = jnp.sum(need_f, axis=1, keepdims=True)
     units = jnp.floor((count + (UNIT - 1)) * (1.0 / UNIT))
@@ -132,33 +139,26 @@
     for copy in copies:
         copy.start()
 
-    x_s[...] = jnp.zeros_like(x_s)
-    dep_s[...] = jnp.zeros_like(dep_s)
-    a_buf[...] = jnp.zeros_like(a_buf)
-    b_buf[...] = jnp.zeros_like(b_buf)
-
-    def part(ref, b, h):
-        return ref[pl.ds(b, 1), :][:, h * LANES : (h + 1) * LANES]
-
-    def given(field, b, h):
-        at = field * events + h * LANES
-        return g_ref[b, 0:1, at : at + LANES]
+    def row_of(b):
+        def part(field, h):
+            return all_s[field, pl.ds(b, 1), :][:, h * LANES : (h + 1) * LANES]
+
+        return part
 
     def lane_sums(t_i, r_i, c_i, b, before):
         total = None
         for back in range(NB + 1):
-            near = b if back == 0 else jnp.maximum(b - back, 0)
-            s = b if back == 0 else jnp.where(b >= back, b - back, blocks)
+            part = row_of(b if back == 0 else jnp.where(b >= back, b - back, blocks))
             for h in range(halves):
-                gap = (t_i - part(t_s, s, h)) + omori_offset
-                dr = r_i - given(1, near, h)
-                dc = c_i - given(2, near, h)
-                expo = (part(l_s, s, h) - (omori_power * LOG2E) * jnp.log(gap)) - (
+                gap = (t_i - part(T, h)) + omori_offset
+                dr = r_i - part(R, h)
+                dc = c_i - part(C, h)
+                expo = (part(L, h) - (omori_power * LOG2E) * jnp.log(gap)) - (
                     dr * dr + dc * dc
-                ) * part(v_s, near, h)
+                ) * part(V, h)
                 term = jnp.exp2(expo)
                 if back == 0:
-                    term = jnp.where(before(h), term, 0.0)
+                    term = jnp.where(before(part, h), term, 0.0)
                 total = term if total is None else total + term
         return jnp.sum(total, axis=1, keepdims=True)
 
@@ -172,23 +172,30 @@
     for k in range(3):
         own_s[k] = jnp.broadcast_to(own_cols[:, k : k + 1], (events, LANES))
 
+    own_steps = events // (OWN_STEP * UNIT)
+    dep_s[...] = jnp.zeros_like(dep_s)
+
     def own_step(k, found):
-        for j in range(STEP):
-            at = k * (STEP * UNIT) + j * UNIT
+        for ref, first, size in ((x_s, 8, M_ROWS), (a_buf, 0, a_buf.shape[0]), (b_buf, 0, b_buf.shape[0])):
+            size = size // own_steps
+            at = pl.ds(pl.multiple_of(first + k * size, 8), size)
+            ref[at] = jnp.zeros((size, ref.shape[1]), ref.dtype)
+        for j in range(OWN_STEP):
+            at = k * (OWN_STEP * UNIT) + j * UNIT
             target = sub_f + at.astype(f32)
             t_i, r_i, c_i = (own_s[n, pl.ds(pl.multiple_of(at, UNIT), UNIT)] for n in range(3))
-            trig = lane_sums(t_i, r_i, c_i, own, lambda h: lane_f + h * LANES < target)
+            trig = lane_sums(t_i, r_i, c_i, own, lambda part, h: lane_f + h * LANES < target)
             found = tuple(
                 found[h] + jnp.where(lane_f + h * LANES == target, trig, 0.0) for h in range(halves)
             )
         return found
 
     found = lax.fori_loop(
-        0, events // (STEP * UNIT), own_step, tuple(jnp.zeros((UNIT, LANES), f32) for _ in range(halves))
+        0, own_steps, own_step, tuple(jnp.zeros((UNIT, LANES), f32) for _ in range(halves))
     )
     for h in range(halves):
         trig = jnp.sum(found[h], axis=0, keepdims=True)
-        logint_ref[:, h * LANES : (h + 1) * LANES] = jnp.log(given(4, own, h) + trig)
+        logint_ref[:, h * LANES : (h + 1) * LANES] = jnp.log(row_of(own)(B, h) + trig)
 
     for copy in copies:
         copy.wait()
@@ -236,7 +243,7 @@
             order = rank + fst_s[0, u]
             at = slice(j * UNIT, (j + 1) * UNIT)
             t_i, r_i, c_i = sel_s[0, at], sel_s[1, at], sel_s[2, at]
-            trig = lane_sums(t_i, r_i, c_i, b, lambda h: part(pos_s, b, h) < order)
+            trig = lane_sums(t_i, r_i, c_i, b, lambda part, h: part(RANK, h) < order)
             dep_s[0, at] = r_i
             dep_s[1, at] = c_i
             dep_s[2, at] = sel_s[3, at]
@@ -247,11 +254,12 @@
             u = i * STEP + j
             b = blk_s[0, u]
             order = rank + fst_s[0, u]
-            picks = [part(posm_s, b, h) == order for h in range(halves)]
-            for k, field in enumerate((0, 1, 2, 4)):
+            part = row_of(b)
+            picks = [part(PICK, h) == order for h in range(halves)]
+            for k, field in enumerate((T, R, C, B)):
                 value = None
                 for h in range(halves):
-                    piece = jnp.where(picks[h], given(field, b, h), 0.0)
+                    piece = jnp.where(picks[h], part(field, h), 0.0)
                     value = piece if value is None else value + piece
                 value = jnp.sum(value, axis=1, keepdims=True)
                 sel_s[k, j * UNIT : (j + 1) * UNIT] = jnp.broadcast_to(value, (UNIT, LANES))
@@ -282,11 +290,11 @@
     span = LATITUDE_SPAN
     wide = LO_COLS // LANES
     middle = (col_blocks // 2) * LO_COLS
-    zeros = jnp.zeros((span, LO_COLS), f32)
-    x_s[0:8] = jnp.concatenate([zeros, x_s[M_ROWS : M_ROWS + span]])
-    x_s[8 + M_ROWS : 16 + M_ROWS] = jnp.concatenate([x_s[8 + span : 16], zeros])
+    edge = jnp.zeros((span, LO_COLS), f32)
+    x_s[0:8] = jnp.concatenate([edge, x_s[M_ROWS : M_ROWS + span]])
+    x_s[8 + M_ROWS : 16 + M_ROWS] = jnp.concatenate([x_s[8 + span : 16], edge])
     lane_t = lax.broadcasted_iota(i32, (8, LANES), 1)
-    per = 4
+    per = PER
 
     def columns(g, carry):
         for p in range(per):
@@ -330,8 +338,6 @@
     )(*rows)
     gathered = lax.all_to_all(spread_out, AXES, 0, 0, tiled=True)
     listed = blocks * events // UNIT + LANES
-    padded = pltpu.VMEM((blocks + 8, events), f32)
-    field = pltpu.VMEM((blocks, events), f32)
     log_intensity, density = pl.pallas_call(
         kernel,
         out_shape=(
@@ -341,7 +347,7 @@
         in_specs=[vmem, vmem, vmem],
         out_specs=(vmem, vmem),
         scratch_shapes=[
-            padded, padded, field, field, field,
+            pltpu.VMEM((FIELDS, blocks + 8, events), f32),
             pltpu.VMEM((3, events, LANES), f32),
             pltpu.VMEM((1, listed), jnp.int32),
             pltpu.VMEM((1, listed), f32),

time: 24.4 us -> 23.2 us (0.951)
  Pallas kernels: 6.58 us -> 5.35 us
    pallas_call x1, Pallas kernels: 6.53 us -> 5.31 us  [body(): pl.pallas_call(kernel, out_shape=(jax.ShapeDtypeStruct((1, events), f32),...]
where the time goes in v4:
time: 23.2 us; the launch traced here: 23 us
  blocking collectives  16.2 us (70%)
  Pallas kernels  5.35 us (23%)
  local copies, waits for them, and re-layouts  0.7 us (3%)
  between operations  0.7 us (3%)
    all_to_all x1, blocking collectives, body(): gathered = lax.all_to_all(spread_out, AXES, 0, 0, tiled=True)  16.2 us
    pallas_call x1, Pallas kernels, body(): pl.pallas_call(kernel, out_shape=(jax.ShapeDtypeStruct((1, events), f32),...  5.31 us
    unnamed x14, local copies, waits for them, and re-layouts  0.7 us

profile of v4, /device:TPU:0, one launch (start us, length us, event | category | flops | bytes accessed | tf_op | source)
XLA Modules:
  0.0 23.0 jit_solution(16816947590785128972)
XLA Ops:
  0.6 0.0 copy-start.6
  0.6 0.0 copy-start.3
  0.7 0.0 copy-start.4
  0.7 0.0 copy-start.1
  0.7 0.0 copy-start.2
  0.7 0.0 copy-start
  0.7 0.0 copy-start.5
  0.7 0.6 %copy-done.6 = f32[8]{0:T(128)S(1)} copy-done((f32[8]{0:T(128)S(1)}, f32[8]{0:T(128)}, u32[]{:S(2)}) %copy-start.6) | copy-done | bytes 56
  1.3 0.0 copy-done.3
  1.3 0.0 copy-done.4
  1.3 0.0 copy-done.1
  1.4 0.0 copy-done.2
  1.4 0.0 copy-done
  1.4 0.0 copy-done.5
  1.4 16.2 %all_to_all.5.g_ref = f32[32,1,1280]{2,1,0:T(1,128)S(1)} all-to-all(f32[32,1,1280]{2,1,0:T(1,128)S(1)} %get-tuple-element.7), channel_id=1, replica_groups=mesh['tm'=16,'grid'=2] {'tm','grid'}, dimensions={0} | all-to-all | bytes 327680 | tf_op jit(solution)/shard_map/all_to_all | solution.py:339
  17.7 5.3 %shard_map.87 = (f32[1,256]{1,0:T(1,128)}, f32[4,16384]{1,0:T(4,128)}) custom-call(f32[32,1,1280]{2,1,0:T(1,128)S(1)} %all_to_all.5.g_ref, f32[1,8]{1,0:T(1,128)S(1)} %get-tuple-element.8.lof_ref, f32[1,8]{1,0:T(1,128)S(1)} %get-tuple-element.9.vof_ref), custom_call_target="tpu_custom_call" | custom-call | tf_op jit(solution)/shard_map/pallas_call | solution.py:341
  (1 shorter events, 0.0 us)
Async XLA Ops:
  0.6 0.7 %copy-start.6 = (f32[8]{0:T(128)S(1)}, f32[8]{0:T(128)}, u32[]{:S(2)}) copy-start(f32[8]{0:T(128)} %param.13) | copy-start | bytes 100
  0.6 0.7 %copy-start.3 = (s32[256]{0:T(256)S(1)}, s32[256]{0:T(256)}, u32[]{:S(2)}) copy-start(s32[256]{0:T(256)} %param.10) | copy-start | bytes 3076
  0.7 0.7 %copy-start.4 = (f32[256]{0:T(256)S(1)}, f32[256]{0:T(256)}, u32[]{:S(2)}) copy-start(f32[256]{0:T(256)} %param.11) | copy-start | bytes 3076
  0.7 0.7 %copy-start.1 = (s32[256]{0:T(256)S(1)}, s32[256]{0:T(256)}, u32[]{:S(2)}) copy-start(s32[256]{0:T(256)} %param.8) | copy-start | bytes 3076
  0.7 0.7 %copy-start.2 = (s32[256]{0:T(256)S(1)}, s32[256]{0:T(256)}, u32[]{:S(2)}) copy-start(s32[256]{0:T(256)} %param.9) | copy-start | bytes 3076
  0.7 0.7 %copy-start = (f32[256]{0:T(256)S(1)}, f32[256]{0:T(256)}, u32[]{:S(2)}) copy-start(f32[256]{0:T(256)} %param.7) | copy-start | bytes 3076
  0.7 0.7 %copy-start.5 = (f32[8]{0:T(128)S(1)}, f32[8]{0:T(128)}, u32[]{:S(2)}) copy-start(f32[8]{0:T(128)} %param.12) | copy-start | bytes 100
